TPU v7x, 128 devices: a whole 4x4x4 slice. The times are simulated.
128 devices in a mesh: frame: 8 (over x_hi, z), pos: 16 (over y, x_lo, core).
Axes of the slice: x: 4 (x_hi: 2, x_lo: 2; x = x_hi * 2 + x_lo), y: 4, z: 4, core: 2. Of those that a mesh axis runs over, the one named last changes fastest.
Arguments:
- latents: bfloat16 [256, 1024, 256], P('frame', 'pos'), as said below
- gain_one: float32 [256], replicated, may hold values from 0.5 to 1.5
- query_one: bfloat16 [256, 256], replicated, as said below
- key_one: bfloat16 [256, 256], replicated, as said below
- value_one: bfloat16 [256, 256], replicated, may hold values from -0.375 to 0.375
- out_one: bfloat16 [256, 256], replicated, may hold values from -0.75 to 0.75
- gain_two: float32 [256], replicated, may hold values from 0.5 to 1.5
- query_two: bfloat16 [256, 256], replicated, as said below
- key_two: bfloat16 [256, 256], replicated, as said below
- value_two: bfloat16 [256, 256], replicated, may hold values from -0.375 to 0.375
- out_two: bfloat16 [256, 256], replicated, may hold values from -0.75 to 0.75
Outputs:
- decoded: bfloat16 [256, 1024, 256], P('frame', 'pos')
Inputs may be any that keep to these rules, and one draw needn't show every extreme that they name: `latents`: latent features of the video. `query_one`: A projection of the spatial block. `key_one`: A projection of the spatial block. `query_two`: A projection of the temporal block. `key_two`: A projection of the temporal block.
All inputs are finite; a program needn't handle non-finite values.
Results may differ from a plain program's by a relative error of at most 0.015.
The roundings to bfloat16 on the way count: a program that leaves them out, or rounds other values in their place, can miss the bound.
Values may be sent and summed in bfloat16 or wider, within the bound.
A program may use at most 320 MiB of HBM per device.

v0:
```python
import jax
import jax.numpy as jnp
from jax import lax
from jax.sharding import PartitionSpec as P

HEADS = 4


def normed(values, gain):
    wide = values.astype(jnp.float32)
    factor = lax.rsqrt(jnp.mean(wide * wide, axis=-1, keepdims=True) + 1e-06)
    return (wide * factor * gain).astype(jnp.bfloat16)


def project(values, weight):
    flat = values.reshape(-1, values.shape[-1])
    result = jnp.dot(flat, weight, preferred_element_type=jnp.float32).astype(jnp.bfloat16)
    return result.reshape(values.shape[:-1] + (weight.shape[1],))


def heads_of(values):
    return values.reshape(values.shape[:-1] + (HEADS, values.shape[-1] // HEADS))


def softmax_attend(query, keys, vals, score_form, value_form, total_form):
    scale = query.shape[-1] ** (-0.5)
    scores = jnp.einsum(score_form, query, keys, preferred_element_type=jnp.float32) * scale
    weights = jnp.exp(scores - jnp.max(scores, axis=-1, keepdims=True))
    totals = jnp.sum(weights, axis=-1)
    summed = jnp.einsum(
        value_form, weights.astype(jnp.bfloat16), vals, preferred_element_type=jnp.float32
    )
    return summed / jnp.einsum(total_form, totals)[..., None]


def shards(
    latents,
    gain_one,
    query_one,
    key_one,
    value_one,
    out_one,
    gain_two,
    query_two,
    key_two,
    value_two,
    out_two,
):
    frames, places, width = latents.shape
    n_pos = lax.axis_size("pos")
    n_frame = lax.axis_size("frame")
    per = frames // n_pos
    first = jnp.where(lax.axis_index("frame") == 0, latents[0], 0).astype(latents.dtype)
    first = lax.psum(first, "frame")
    sent = jnp.concatenate(
        [
            latents.reshape(n_pos, per, places, width),
            jnp.broadcast_to(first[None, None], (n_pos, 1, places, width)),
        ],
        axis=1,
    )
    got = lax.all_to_all(sent, "pos", 0, 0, tiled=True)
    xs = got[:, :per].transpose(1, 0, 2, 3).reshape(per, n_pos * places, width)
    x0 = got[:, per].reshape(n_pos * places, width)
    n_one = normed(xs, gain_one)
    q_one = heads_of(project(n_one, query_one))
    k_one = heads_of(project(n_one, key_one))
    v_one = heads_of(project(n_one, value_one))
    n_zero = normed(x0, gain_one)
    k_zero = heads_of(project(n_zero, key_one))
    v_zero = heads_of(project(n_zero, value_one))
    keys = jnp.concatenate([k_one, jnp.broadcast_to(k_zero[None], k_one.shape)], axis=1)
    vals = jnp.concatenate([v_one, jnp.broadcast_to(v_zero[None], v_one.shape)], axis=1)
    attended_one = (
        softmax_attend(q_one, keys, vals, "fphd,fkhd->fhpk", "fhpk,fkhd->fphd", "fhp->fph")
        .reshape(xs.shape)
        .astype(jnp.bfloat16)
    )
    mixed_one = jnp.dot(
        attended_one.reshape(-1, width), out_one, preferred_element_type=jnp.float32
    ).reshape(xs.shape)
    middle = (xs.astype(jnp.float32) + mixed_one).astype(jnp.bfloat16)
    all_places = n_pos * places
    run = all_places // (n_pos * n_frame)
    sent = (
        middle.reshape(per, n_pos, n_frame, run, width)
        .transpose(2, 1, 0, 3, 4)
        .reshape(n_frame * n_pos, per, run, width)
    )
    got = lax.all_to_all(sent, ("frame", "pos"), 0, 0, tiled=True)
    mid_t = got.reshape(n_frame * n_pos * per, run, width)
    n_two = normed(mid_t, gain_two)
    q_two = heads_of(project(n_two, query_two))
    k_two = heads_of(project(n_two, key_two))
    v_two = heads_of(project(n_two, value_two))
    attended_two = (
        softmax_attend(q_two, k_two, v_two, "fphd,kphd->phfk", "phfk,kphd->fphd", "phf->fph")
        .reshape(mid_t.shape)
        .astype(jnp.bfloat16)
    )
    mixed_two = jnp.dot(
        attended_two.reshape(-1, width), out_two, preferred_element_type=jnp.float32
    ).reshape(mid_t.shape)
    decoded = (mid_t.astype(jnp.float32) + mixed_two).astype(jnp.bfloat16)
    sent = decoded.reshape(n_frame, frames, run, width)
    got = lax.all_to_all(sent, "frame", 0, 0, tiled=True)
    return got.transpose(1, 0, 2, 3).reshape(frames, places, width)


def solution(mesh):
    return jax.shard_map(
        shards,
        mesh=mesh,
        in_specs=(P("frame", "pos", None), P(), P(), P(), P(), P(), P(), P(), P(), P(), P()),
        out_specs=P("frame", "pos", None),
        check_vma=False,
    )
```

profile of v0, /device:TPU:0, one launch (start us, length us, event | category | flops | bytes accessed | tf_op | source)
XLA Modules:
  0.0 243.1 jit_solution(5843305531094082782)
XLA Ops:
  0.0 0.8 select_bitcast_fusion
  0.8 43.1 %psum.7 = bf16[64,256]{1,0:T(8,128)(2,1)S(1)} all-reduce(bf16[64,256]{1,0:T(8,128)(2,1)S(1)} %select_bitcast_fusion), channel_id=1, replica_groups=mesh['frame'=8,'pos'=16] {'frame'}, use_global_device_ids=true, to_apply=%region_0.1 | all-reduce | flops 16384 | bytes 65536 | tf_op jit(solution)/shard_map/psum | solution.py:54
  44.0 1.4 pad_maximum_fusion
  45.3 26.5 %all_to_all.15 = bf16[16,3,64,256]{3,2,1,0:T(8,128)(2,1)S(1)} all-to-all(bf16[16,3,64,256]{3,2,1,0:T(8,128)(2,1)S(1)} %pad_maximum_fusion), channel_id=1, replica_groups=mesh['frame'=8,'pos'=16] {'pos'}, dimensions={0} | all-to-all | bytes 3145728 | tf_op jit(solution)/shard_map/all_to_all | solution.py:62
  71.9 0.3 multiply_reduce_fusion.3
  72.3 0.2 multiply_reduce_fusion.4
  72.5 0.5 copy-done.1
  73.1 1.5 copy_convert_fusion
  74.6 0.3 fusion.18
  74.9 1.4 convolution_convert_fusion.3
  76.3 1.2 slice_convert_fusion
  77.5 0.2 fusion.35
  77.7 1.1 convolution_convert_fusion.6
  78.9 1.4 convolution_convert_fusion.5
  80.3 1.1 convolution_convert_fusion.7
  81.4 4.5 %reshape.135 = bf16[2,1024,4,64]{3,2,1,0:T(4,128)(2,1)} reshape(bf16[2048,256]{1,0:T(8,128)(2,1)} %convolution_convert_fusion.3) | data formatting | bytes 2097152 | tf_op jit(solution)/shard_map/reshape;reshape | solution.py:22
  85.9 4.1 %copy.61 = bf16[2,1024,4,64]{1,3,2,0:T(8,128)(2,1)} copy(bf16[2,1024,4,64]{3,2,1,0:T(4,128)(2,1)} %reshape.135) | data formatting | bytes 2097152 | tf_op jit(solution)/shard_map/reshape;reshape | solution.py:22
  89.9 1.4 convolution_convert_fusion.4
  91.4 4.5 %reshape.134 = bf16[2,1024,4,64]{3,2,1,0:T(4,128)(2,1)} reshape(bf16[2048,256]{1,0:T(8,128)(2,1)} %convolution_convert_fusion.4) | data formatting | bytes 2097152 | tf_op jit(solution)/shard_map/reshape;reshape | solution.py:22
  95.9 1.9 reshape.133
  97.8 4.2 %copy.58 = bf16[2,1024,4,64]{1,3,2,0:T(8,128)(2,1)} copy(bf16[2,1024,4,64]{3,2,1,0:T(4,128)(2,1)} %reshape.133) | data formatting | bytes 2097152 | tf_op jit(solution)/shard_map/reshape;reshape | solution.py:22
  101.9 1.2 broadcast_in_dim.19
  103.1 24.7 %multiply_reduce_fusion = (f32[2,4,1024]{2,1,0:T(4,128)S(1)}, f32[2,4,1024,2048]{3,2,1,0:T(8,128)}) fusion(bf16[2,1024,4,64]{1,3,2,0:T(8,128)(2,1)S(1)} %broadcast_in_dim.19, bf16[2,1024,4,64]{1,3,2,0:T(8,128)(2,1)S(1)} %copy-done.3, bf16[2,1024,4,64]{3,2,1,0:T(4,128)(2,1)} %reshape.134), kind=kOutput, calls=%fused_computation.1 | convolution fusion | flops 2185224192 | bytes 70287360 | tf_op jit(solution)/shard_map/fphd,fkhd->fhpk/dot_general | solution.py:27
  127.8 21.2 %fusion = f32[2,4,1024]{2,1,0:T(4,128)S(1)} fusion(f32[2,4,1024,2048]{3,2,1,0:T(8,128)} %get-tuple-element.6, f32[2,4,1024]{2,1,0:T(4,128)S(1)} %get-tuple-element.5), kind=kLoop, calls=%fused_computation.2 | loop fusion | flops 50323456 | bytes 67174400 | tf_op jit(solution)/shard_map/reduce_sum | solution.py:29
  149.1 2.2 broadcast_in_dim.17
  151.3 24.9 %fusion.24 = bf16[2,1024,4,64]{1,3,2,0:T(8,128)(2,1)} fusion(f32[2,4,1024,2048]{3,2,1,0:T(8,128)} %get-tuple-element.6, f32[2,4,1024]{2,1,0:T(4,128)S(1)} %get-tuple-element.5, bf16[2,1024,4,64]{1,3,2,0:T(8,128)(2,1)} %broadcast_in_dim.17, bf16[2,1024,4,64]{1,3,2,0:T(8,128)(2,1)S(1)} %copy-done.4, f32[2,1024,4]{1,2,0:T(4,128)S(1)} %bitcast.88), kind=kOutput, calls=%fused_computation.38 | convolution fusion | flops 2203058176 | bytes 70320128 | tf_op jit(solution)/shard_map/fhpk,fkhd->fphd/dot_general | solution.py:30
  176.3 1.7 fusion.19
  178.0 0.1 copy.64
  178.1 23.2 %all_to_all.16 = bf16[128,2,8,256]{3,2,1,0:T(8,128)(2,1)S(1)} all-to-all(bf16[128,2,8,256]{3,2,1,0:T(8,128)(2,1)S(1)} %bitcast.80), channel_id=1, replica_groups=mesh['frame'=8,'pos'=16] {'frame','pos'}, dimensions={0} | all-to-all | bytes 2097152 | tf_op jit(solution)/shard_map/all_to_all | solution.py:90
  201.3 0.5 multiply_reduce_fusion.2
  201.7 0.1 add_rsqrt_fusion
  201.8 0.2 rsqrt.38
  202.0 0.3 fusion.22
  202.4 0.4 convolution_convert_fusion.1
  202.8 1.8 reshape_reshape.22
  204.7 0.4 convolution_convert_fusion
  205.1 1.9 reshape_reshape.23
  207.0 1.4 convolution_convert_fusion.2
  208.4 4.6 %reshape_reshape.21 = bf16[256,8,4,64]{3,2,1,0:T(4,128)(2,1)} reshape(bf16[2048,256]{1,0:T(8,128)(2,1)} %convolution_convert_fusion.2) | data formatting | bytes 2097152 | tf_op jit(solution)/shard_map/reshape;reshape | solution.py:22
  213.0 3.6 %multiply_reduce_fusion.1 = (f32[8,4,256]{2,1,0:T(4,128)S(1)}, f32[8,4,256,256]{2,3,1,0:T(8,128)S(1)}) fusion(bf16[256,8,4,64]{3,2,1,0:T(4,128)(2,1)} %reshape_reshape.23, bf16[256,8,4,64]{3,2,1,0:T(4,128)(2,1)S(1)} %copy-done.2), kind=kOutput, calls=%fused_computation.6 | convolution fusion | flops 272621568 | bytes 10518528 | tf_op jit(solution)/shard_map/fphd,kphd->phfk/dot_general | solution.py:27
  216.6 1.5 fusion.4
  218.2 1.9 fusion.20
  220.1 0.2 bitcast_convert_fusion
  220.3 0.7 copy-done.13
  221.0 0.9 fusion.23
  221.9 0.1 copy.71
  222.0 19.6 %all_to_all.17 = bf16[8,32,8,256]{3,1,2,0:T(8,128)(2,1)S(1)} all-to-all(bf16[8,32,8,256]{3,1,2,0:T(8,128)(2,1)S(1)} %copy.71), channel_id=1, replica_groups=mesh['frame'=8,'pos'=16] {'frame'}, dimensions={0} | all-to-all | bytes 2097152 | tf_op jit(solution)/shard_map/all_to_all | solution.py:106
  241.6 1.6 copy.72
  (35 shorter events, 0.3 us)
Async XLA Ops:
  0.0 74.9 %copy-start = (bf16[256,256]{1,0:T(8,128)(2,1)S(1)}, bf16[256,256]{1,0:T(8,128)(2,1)}, u32[]{:S(2)}) copy-start(bf16[256,256]{1,0:T(8,128)(2,1)} %param.14) | copy-start | bytes 393220
  71.9 1.2 copy-start.1
  72.2 2.3 copy-start.14
  76.3 2.5 %copy-start.7 = (bf16[256,256]{1,0:T(8,128)(2,1)S(1)}, bf16[256,256]{1,0:T(8,128)(2,1)}, u32[]{:S(2)}) copy-start(bf16[256,256]{1,0:T(8,128)(2,1)} %param.15) | copy-start | bytes 393220
  85.9 4.1 %copy-start.8 = (bf16[256,256]{1,0:T(8,128)(2,1)S(1)}, bf16[256,256]{1,0:T(8,128)(2,1)}, u32[]{:S(2)}) copy-start(bf16[256,256]{1,0:T(8,128)(2,1)} %param.13) | copy-start | bytes 393220
  91.4 4.5 %copy-start.5 = (bf16[2048,256]{1,0:T(8,128)(2,1)S(1)}, bf16[2048,256]{1,0:T(8,128)(2,1)}, u32[]{:S(2)}) copy-start(bf16[2048,256]{1,0:T(8,128)(2,1)} %convolution_convert_fusion.5) | copy-start | bytes 3145732
  97.8 5.3 %copy-start.3 = (bf16[2,1024,4,64]{1,3,2,0:T(8,128)(2,1)S(1)}, bf16[2,1024,4,64]{1,3,2,0:T(8,128)(2,1)}, u32[]{:S(2)}) copy-start(bf16[2,1024,4,64]{1,3,2,0:T(8,128)(2,1)} %copy.61) | copy-start | bytes 3145732
  149.1 2.2 copy-start.4
  151.3 24.9 %copy-start.9 = (bf16[256,256]{1,0:T(8,128)(2,1)S(1)}, bf16[256,256]{1,0:T(8,128)(2,1)}, u32[]{:S(2)}) copy-start(bf16[256,256]{1,0:T(8,128)(2,1)} %param.16) | copy-start | bytes 393220
  178.1 24.0 %copy-start.15 = (f32[256]{0:T(256)S(1)}, f32[256]{0:T(256)}, u32[]{:S(2)}) copy-start(f32[256]{0:T(256)} %param.17) | copy-start | bytes 3076
  201.3 1.1 copy-start.10
  202.8 1.8 copy-start.11
  205.1 1.9 copy-start.12
  208.4 4.6 %copy-start.2 = (bf16[256,8,4,64]{3,2,1,0:T(4,128)(2,1)S(1)}, bf16[256,8,4,64]{3,2,1,0:T(4,128)(2,1)}, u32[]{:S(2)}) copy-start(bf16[256,8,4,64]{3,2,1,0:T(4,128)(2,1)} %reshape_reshape.22) | copy-start | bytes 3145732
  216.6 1.6 copy-start.6
  220.1 0.9 copy-start.13
where the time goes:
time: 244 us; the launch traced here: 243 us
  blocking collectives  112 us (46%)
  matrix products  66.5 us (27%)
  local copies, waits for them, and re-layouts  34.1 us (14%)
  other arithmetic  29.8 us (12%)
    psum x1, blocking collectives, shards(): first = lax.psum(first, 'frame')  43.1 us
    dot_general x2, matrix products, softmax_attend(): jnp.einsum(score_form, query, keys, preferred_element_type=jnp.float32)  28.3 us
    another operation x8, local copies, waits for them, and re-layouts, heads_of(): values.reshape(values.shape[:-1] + (HEADS, values.shape[-1] // HEADS))  27.4 us
    dot_general x2, matrix products, softmax_attend(): jnp.einsum(value_form, weights.astype(jnp.bfloat16), vals, preferred_elem...  26.9 us
    all_to_all x1, blocking collectives, shards(): got = lax.all_to_all(sent, 'pos', 0, 0, tiled=True)  26.5 us
    all_to_all x1, blocking collectives, shards(): got = lax.all_to_all(sent, ('frame', 'pos'), 0, 0, tiled=True)  23.2 us
    reduce_sum x2, other arithmetic, softmax_attend(): totals = jnp.sum(weights, axis=-1)  22.8 us
    all_to_all x1, blocking collectives, shards(): got = lax.all_to_all(sent, 'frame', 0, 0, tiled=True)  19.6 us

commit v1 on v0

--- a/solution.py
+++ b/solution.py
@@ -51,7 +51,7 @@
     n_frame = lax.axis_size("frame")
     per = frames // n_pos
     first = jnp.where(lax.axis_index("frame") == 0, latents[0], 0).astype(latents.dtype)
-    first = lax.psum(first, "frame")
+    first = jnp.sum(lax.all_gather(first, "frame"), axis=0)
     sent = jnp.concatenate(
         [
             latents.reshape(n_pos, per, places, width),

time: 244 us -> 241 us (0.988)
  blocking collectives: 112 us -> 109 us
    psum x1 -> x0, blocking collectives: 43.1 us -> none  [shards(): first = lax.psum(first, 'frame')]
    all_gather x0 -> x1, blocking collectives: none -> 35.7 us  [shards(): first = jnp.sum(lax.all_gather(first, 'frame'), axis=0)]
    all_to_all x1, blocking collectives: 23.2 us -> 27.2 us  [shards(): got = lax.all_to_all(sent, ('frame', 'pos'), 0, 0, tiled=True)]
where the time goes in v1:
time: 241 us; the launch traced here: 240 us
  blocking collectives  109 us (45%)
  matrix products  66.5 us (28%)
  local copies, waits for them, and re-layouts  34.1 us (14%)
  other arithmetic  29.9 us (12%)
    all_gather x1, blocking collectives, shards(): first = jnp.sum(lax.all_gather(first, 'frame'), axis=0)  35.7 us
    dot_general x2, matrix products, softmax_attend(): jnp.einsum(score_form, query, keys, preferred_element_type=jnp.float32)  28.3 us
    another operation x8, local copies, waits for them, and re-layouts, heads_of(): values.reshape(values.shape[:-1] + (HEADS, values.shape[-1] // HEADS))  27.4 us
    all_to_all x1, blocking collectives, shards(): got = lax.all_to_all(sent, ('frame', 'pos'), 0, 0, tiled=True)  27.2 us
    dot_general x2, matrix products, softmax_attend(): jnp.einsum(value_form, weights.astype(jnp.bfloat16), vals, preferred_elem...  26.9 us
    all_to_all x1, blocking collectives, shards(): got = lax.all_to_all(sent, 'pos', 0, 0, tiled=True)  26.5 us
    reduce_sum x2, other arithmetic, softmax_attend(): totals = jnp.sum(weights, axis=-1)  22.8 us
    all_to_all x1, blocking collectives, shards(): got = lax.all_to_all(sent, 'frame', 0, 0, tiled=True)  19.6 us

profile of v1, /device:TPU:0, one launch (start us, length us, event | category | flops | bytes accessed | tf_op | source)
XLA Modules:
  0.0 239.8 jit_solution(6449035921585722603)
XLA Ops:
  0.0 0.8 slice_select_fusion
  0.8 35.7 %all_gather.4 = bf16[8,64,256]{2,1,0:T(8,128)(2,1)S(1)} all-gather(bf16[1,64,256]{2,1,0:T(8,128)(2,1)S(1)} %slice_select_fusion), channel_id=1, replica_groups=mesh['frame'=8,'pos'=16] {'frame'}, dimensions={0}, use_global_device_ids=true | all-gather | bytes 294912 | tf_op jit(solution)/shard_map/all_gather | solution.py:54
  36.6 1.4 pad_maximum_fusion
  38.0 26.5 %all_to_all.15 = bf16[16,3,64,256]{3,2,1,0:T(8,128)(2,1)S(1)} all-to-all(bf16[16,3,64,256]{3,2,1,0:T(8,128)(2,1)S(1)} %pad_maximum_fusion), channel_id=1, replica_groups=mesh['frame'=8,'pos'=16] {'pos'}, dimensions={0} | all-to-all | bytes 3145728 | tf_op jit(solution)/shard_map/all_to_all | solution.py:62
  64.5 0.3 multiply_reduce_fusion.3
  65.0 0.2 multiply_reduce_fusion.4
  65.2 0.5 copy-done.1
  65.7 1.5 copy_convert_fusion
  67.2 0.3 fusion.18
  67.6 1.4 convolution_convert_fusion.3
  69.0 1.2 slice_convert_fusion
  70.2 0.2 fusion.35
  70.4 1.1 convolution_convert_fusion.6
  71.5 1.4 convolution_convert_fusion.5
  72.9 1.1 convolution_convert_fusion.7
  74.1 4.5 %reshape.132 = bf16[2,1024,4,64]{3,2,1,0:T(4,128)(2,1)} reshape(bf16[2048,256]{1,0:T(8,128)(2,1)} %convolution_convert_fusion.3) | data formatting | bytes 2097152 | tf_op jit(solution)/shard_map/reshape;reshape | solution.py:22
  78.5 4.1 %copy.61 = bf16[2,1024,4,64]{1,3,2,0:T(8,128)(2,1)} copy(bf16[2,1024,4,64]{3,2,1,0:T(4,128)(2,1)} %reshape.132) | data formatting | bytes 2097152 | tf_op jit(solution)/shard_map/reshape;reshape | solution.py:22
  82.6 1.4 convolution_convert_fusion.4
  84.0 4.5 %reshape.131 = bf16[2,1024,4,64]{3,2,1,0:T(4,128)(2,1)} reshape(bf16[2048,256]{1,0:T(8,128)(2,1)} %convolution_convert_fusion.4) | data formatting | bytes 2097152 | tf_op jit(solution)/shard_map/reshape;reshape | solution.py:22
  88.6 1.9 reshape.130
  90.4 4.2 %copy.58 = bf16[2,1024,4,64]{1,3,2,0:T(8,128)(2,1)} copy(bf16[2,1024,4,64]{3,2,1,0:T(4,128)(2,1)} %reshape.130) | data formatting | bytes 2097152 | tf_op jit(solution)/shard_map/reshape;reshape | solution.py:22
  94.6 1.2 broadcast_in_dim.19
  95.8 24.7 %multiply_reduce_fusion = (f32[2,4,1024]{2,1,0:T(4,128)S(1)}, f32[2,4,1024,2048]{3,2,1,0:T(8,128)}) fusion(bf16[2,1024,4,64]{1,3,2,0:T(8,128)(2,1)S(1)} %broadcast_in_dim.19, bf16[2,1024,4,64]{1,3,2,0:T(8,128)(2,1)S(1)} %copy-done.3, bf16[2,1024,4,64]{3,2,1,0:T(4,128)(2,1)} %reshape.131), kind=kOutput, calls=%fused_computation.1 | convolution fusion | flops 2185224192 | bytes 70287360 | tf_op jit(solution)/shard_map/fphd,fkhd->fhpk/dot_general | solution.py:27
  120.5 21.2 %fusion = f32[2,4,1024]{2,1,0:T(4,128)S(1)} fusion(f32[2,4,1024,2048]{3,2,1,0:T(8,128)} %get-tuple-element.6, f32[2,4,1024]{2,1,0:T(4,128)S(1)} %get-tuple-element.5), kind=kLoop, calls=%fused_computation.2 | loop fusion | flops 50323456 | bytes 67174400 | tf_op jit(solution)/shard_map/reduce_sum | solution.py:29
  141.8 2.2 broadcast_in_dim.17
  144.0 24.9 %fusion.24 = bf16[2,1024,4,64]{1,3,2,0:T(8,128)(2,1)} fusion(f32[2,4,1024,2048]{3,2,1,0:T(8,128)} %get-tuple-element.6, f32[2,4,1024]{2,1,0:T(4,128)S(1)} %get-tuple-element.5, bf16[2,1024,4,64]{1,3,2,0:T(8,128)(2,1)} %broadcast_in_dim.17, bf16[2,1024,4,64]{1,3,2,0:T(8,128)(2,1)S(1)} %copy-done.4, f32[2,1024,4]{1,2,0:T(4,128)S(1)} %bitcast.86), kind=kOutput, calls=%fused_computation.38 | convolution fusion | flops 2203058176 | bytes 70320128 | tf_op jit(solution)/shard_map/fhpk,fkhd->fphd/dot_general | solution.py:30
  168.9 1.7 fusion.19
  170.7 0.1 copy.64
  170.8 27.2 %all_to_all.16 = bf16[128,2,8,256]{3,2,1,0:T(8,128)(2,1)S(1)} all-to-all(bf16[128,2,8,256]{3,2,1,0:T(8,128)(2,1)S(1)} %bitcast.78), channel_id=1, replica_groups=mesh['frame'=8,'pos'=16] {'frame','pos'}, dimensions={0} | all-to-all | bytes 2097152 | tf_op jit(solution)/shard_map/all_to_all | solution.py:90
  197.9 0.5 multiply_reduce_fusion.2
  198.4 0.1 add_rsqrt_fusion
  198.5 0.2 rsqrt.38
  198.7 0.3 fusion.22
  199.1 0.4 convolution_convert_fusion.1
  199.5 1.8 reshape_reshape.22
  201.3 0.4 convolution_convert_fusion
  201.8 1.9 reshape_reshape.23
  203.7 1.4 convolution_convert_fusion.2
  205.1 4.6 %reshape_reshape.21 = bf16[256,8,4,64]{3,2,1,0:T(4,128)(2,1)} reshape(bf16[2048,256]{1,0:T(8,128)(2,1)} %convolution_convert_fusion.2) | data formatting | bytes 2097152 | tf_op jit(solution)/shard_map/reshape;reshape | solution.py:22
  209.7 3.6 %multiply_reduce_fusion.1 = (f32[8,4,256]{2,1,0:T(4,128)S(1)}, f32[8,4,256,256]{2,3,1,0:T(8,128)S(1)}) fusion(bf16[256,8,4,64]{3,2,1,0:T(4,128)(2,1)} %reshape_reshape.23, bf16[256,8,4,64]{3,2,1,0:T(4,128)(2,1)S(1)} %copy-done.2), kind=kOutput, calls=%fused_computation.6 | convolution fusion | flops 272621568 | bytes 10518528 | tf_op jit(solution)/shard_map/fphd,kphd->phfk/dot_general | solution.py:27
  213.2 1.5 fusion.4
  214.8 1.9 fusion.20
  216.8 0.2 bitcast_convert_fusion
  217.0 0.7 copy-done.13
  217.7 0.9 fusion.23
  218.6 0.1 copy.71
  218.7 19.6 %all_to_all.17 = bf16[8,32,8,256]{3,1,2,0:T(8,128)(2,1)S(1)} all-to-all(bf16[8,32,8,256]{3,1,2,0:T(8,128)(2,1)S(1)} %copy.71), channel_id=1, replica_groups=mesh['frame'=8,'pos'=16] {'frame'}, dimensions={0} | all-to-all | bytes 2097152 | tf_op jit(solution)/shard_map/all_to_all | solution.py:106
  238.2 1.6 copy.72
  (36 shorter events, 0.4 us)
Async XLA Ops:
  0.0 67.6 %copy-start = (bf16[256,256]{1,0:T(8,128)(2,1)S(1)}, bf16[256,256]{1,0:T(8,128)(2,1)}, u32[]{:S(2)}) copy-start(bf16[256,256]{1,0:T(8,128)(2,1)} %param.14) | copy-start | bytes 393220
  64.5 1.2 copy-start.1
  64.9 2.3 copy-start.14
  69.0 2.5 %copy-start.7 = (bf16[256,256]{1,0:T(8,128)(2,1)S(1)}, bf16[256,256]{1,0:T(8,128)(2,1)}, u32[]{:S(2)}) copy-start(bf16[256,256]{1,0:T(8,128)(2,1)} %param.15) | copy-start | bytes 393220
  78.5 4.1 %copy-start.8 = (bf16[256,256]{1,0:T(8,128)(2,1)S(1)}, bf16[256,256]{1,0:T(8,128)(2,1)}, u32[]{:S(2)}) copy-start(bf16[256,256]{1,0:T(8,128)(2,1)} %param.13) | copy-start | bytes 393220
  84.0 4.5 %copy-start.5 = (bf16[2048,256]{1,0:T(8,128)(2,1)S(1)}, bf16[2048,256]{1,0:T(8,128)(2,1)}, u32[]{:S(2)}) copy-start(bf16[2048,256]{1,0:T(8,128)(2,1)} %convolution_convert_fusion.5) | copy-start | bytes 3145732
  90.4 5.3 %copy-start.3 = (bf16[2,1024,4,64]{1,3,2,0:T(8,128)(2,1)S(1)}, bf16[2,1024,4,64]{1,3,2,0:T(8,128)(2,1)}, u32[]{:S(2)}) copy-start(bf16[2,1024,4,64]{1,3,2,0:T(8,128)(2,1)} %copy.61) | copy-start | bytes 3145732
  141.8 2.2 copy-start.4
  144.0 24.9 %copy-start.9 = (bf16[256,256]{1,0:T(8,128)(2,1)S(1)}, bf16[256,256]{1,0:T(8,128)(2,1)}, u32[]{:S(2)}) copy-start(bf16[256,256]{1,0:T(8,128)(2,1)} %param.16) | copy-start | bytes 393220
  170.8 28.0 %copy-start.15 = (f32[256]{0:T(256)S(1)}, f32[256]{0:T(256)}, u32[]{:S(2)}) copy-start(f32[256]{0:T(256)} %param.17) | copy-start | bytes 3076
  197.9 1.1 copy-start.10
  199.5 1.8 copy-start.11
  201.8 1.9 copy-start.12
  205.1 4.6 %copy-start.2 = (bf16[256,8,4,64]{3,2,1,0:T(4,128)(2,1)S(1)}, bf16[256,8,4,64]{3,2,1,0:T(4,128)(2,1)}, u32[]{:S(2)}) copy-start(bf16[256,8,4,64]{3,2,1,0:T(4,128)(2,1)} %reshape_reshape.22) | copy-start | bytes 3145732
  213.2 1.6 copy-start.6
  216.8 0.9 copy-start.13
